TPU v7x, 256 devices: a whole 4x4x8 slice. The times are simulated.
256 devices in a mesh: grp: 8 (over x, core), lx: 4 (over y), ly: 8 (over z).
Axes of the slice: x: 4, y: 4, z: 8, core: 2. Of those that a mesh axis runs over, the one named last changes fastest.
Arguments:
- vectors: float32 [32, 256, 4096], P('grp', 'lx', 'ly'), may hold values from -6 to 6
- levels: int32 [256, 4096], P('lx', 'ly'), may hold values from 0 to 7
- level_table: float32 [8], replicated, may hold values from 1 to 3
- filter_low: float32 [1], replicated, may hold values from -1 to 0.5
- filter_high: float32 [1], replicated, may hold values from 6 to 7.5
Outputs:
- basis: float32 [32, 256, 4096], P('grp', 'lx', 'ly')
All inputs are finite; a program needn't handle non-finite values.
Results may differ from a plain program's by a relative error of at most 0.00011.
Values sent between devices are 32-bit elements; how exact they have to be, the bound alone decides.
No kernel may reach another device: no remote copies, remote signals or barrier semaphores. Data moves between devices by JAX's collectives and lax.ppermute only.
A program may use at most 64 MiB of HBM per device.

v0:
```python
import jax
import jax.numpy as jnp
from jax import lax
from jax.sharding import PartitionSpec as P


def padded_2(shard, sides, width):
    for axis, dim in sides:
        size, length = (lax.axis_size(axis), shard.shape[dim])
        up = [(i, (i + 1) % size) for i in range(size)]
        down = [(j, i) for i, j in up]
        last = lax.slice_in_dim(shard, length - width, length, axis=dim)
        leading = lax.slice_in_dim(shard, 0, width, axis=dim)
        before = lax.ppermute(last, axis, up)
        after = lax.ppermute(leading, axis, down)
        shard = jnp.concatenate([before, shard, after], axis=dim)
    return shard


def from_root(value, axis, source):
    kept = jnp.where(lax.axis_index(axis) == source, value, 0).astype(value.dtype)
    return lax.psum(kept, axis)


def apply_operator(field, onsite):
    padded = padded_2(field, (("lx", 1), ("ly", 2)), 1)
    beside = padded[:, 2:, 1:-1] + padded[:, :-2, 1:-1] + padded[:, 1:-1, 2:] + padded[:, 1:-1, :-2]
    return onsite[None] * field - beside


def lower_inverse(gram):
    lower = jnp.linalg.cholesky(gram)
    eye_block = jnp.eye(gram.shape[0], dtype=jnp.float32)
    return lax.linalg.triangular_solve(lower, eye_block, left_side=True, lower=True)


def body(vectors, levels, level_table, filter_low, filter_high):
    count_vec, rows_local, cols_local = vectors.shape
    level_ids = jnp.arange(level_table.shape[0], dtype=jnp.int32)
    onsite = jnp.sum(
        jnp.where(levels[None] == level_ids[:, None, None], level_table[:, None, None], 0.0), axis=0
    )
    center = (filter_high[0] + filter_low[0]) / 2.0
    half = (filter_high[0] - filter_low[0]) / 2.0
    first = (apply_operator(vectors, onsite) - center * vectors) / half
    filtered = 2.0 * (apply_operator(first, onsite) - center * first) / half - vectors
    total = rows_local * cols_local * lax.axis_size("lx") * lax.axis_size("ly")
    flat = filtered.reshape(count_vec, rows_local * cols_local)
    highest = lax.Precision.HIGHEST
    mine = lax.axis_index("grp")
    result = jnp.zeros_like(flat)
    for h in range(lax.axis_size("grp")):
        gram = lax.psum(jnp.dot(flat, flat.T, precision=highest), ("lx", "ly")) / total
        done = jnp.dot(lower_inverse(gram), flat, precision=highest)
        result = jnp.where(mine == h, done, result)
        shared = from_root(done, "grp", h)
        coeff = lax.psum(jnp.dot(shared, flat.T, precision=highest), ("lx", "ly")) / total
        later = mine > h
        flat = jnp.where(later, flat - jnp.dot(coeff.T, shared, precision=highest), flat)
    return result.reshape(count_vec, rows_local, cols_local)


def solution(mesh):
    in_specs = (P("grp", "lx", "ly"), P("lx", "ly"), P(), P(), P())
    out_specs = P("grp", "lx", "ly")
    return jax.shard_map(body, mesh=mesh, in_specs=in_specs, out_specs=out_specs, check_vma=False)
```

profile of v0, /device:TPU:32, one launch (start us, length us, event | category | flops | bytes accessed | tf_op | source)
XLA Modules:
  0.0 1632.8 jit_solution(7607256732290742390)
XLA Ops:
  11.9 3.5 collective-permute-done.1
  21.7 3.9 collective-permute-done.3
  31.3 3.3 collective-permute-start.6
  42.6 71.0 %psum.154 = f32[4,4]{0,1:T(4,128)S(1)} all-reduce(f32[4,4]{0,1:T(4,128)S(1)} %convolution_bitcast_fusion), channel_id=1, replica_groups=mesh['grp'=8,'lx'=4,'ly'=8] {'lx','ly'}, use_global_device_ids=true, to_apply=%region_1.2 | all-reduce | flops 16 | bytes 128 | tf_op jit(solution)/shard_map/psum | solution.py:53
  118.3 60.3 %all-reduce.8.cloned.1.call-done = f32[4,32768]{1,0:T(4,128)} async-done(((f32[4,32768]{1,0:T(4,128)}), f32[4,32768]{1,0:T(4,128)}) %all-reduce.8.cloned.1.call-update) | async-done | bytes 524304 | tf_op jit(solution)/shard_map/psum | solution.py:22
  178.6 3.5 fusion.99
  182.1 71.6 %psum.156 = f32[4,4]{0,1:T(4,128)S(1)} all-reduce(f32[4,4]{0,1:T(4,128)S(1)} %fusion.99), channel_id=1, replica_groups=mesh['grp'=8,'lx'=4,'ly'=8] {'lx','ly'}, use_global_device_ids=true, to_apply=%region_5.8 | all-reduce | flops 16 | bytes 128 | tf_op jit(solution)/shard_map/psum | solution.py:57
  257.1 73.6 %psum.157 = f32[4,4]{0,1:T(4,128)S(1)} all-reduce(f32[4,4]{0,1:T(4,128)S(1)} %fusion.100), channel_id=1, replica_groups=mesh['grp'=8,'lx'=4,'ly'=8] {'lx','ly'}, use_global_device_ids=true, to_apply=%region_6.9 | all-reduce | flops 16 | bytes 128 | tf_op jit(solution)/shard_map/psum | solution.py:53
  335.0 58.1 %all-reduce.10.cloned.1.call-done = f32[4,32768]{1,0:T(4,128)} async-done(((f32[4,32768]{1,0:T(4,128)}), f32[4,32768]{1,0:T(4,128)}) %all-reduce.10.cloned.1.call-update) | async-done | bytes 524304 | tf_op jit(solution)/shard_map/psum | solution.py:22
  393.1 3.5 fusion.101
  396.6 71.6 %psum.159 = f32[4,4]{0,1:T(4,128)S(1)} all-reduce(f32[4,4]{0,1:T(4,128)S(1)} %fusion.101), channel_id=1, replica_groups=mesh['grp'=8,'lx'=4,'ly'=8] {'lx','ly'}, use_global_device_ids=true, to_apply=%region_8.11 | all-reduce | flops 16 | bytes 128 | tf_op jit(solution)/shard_map/psum | solution.py:57
  471.6 73.6 %psum.160 = f32[4,4]{0,1:T(4,128)S(1)} all-reduce(f32[4,4]{0,1:T(4,128)S(1)} %fusion.102), channel_id=1, replica_groups=mesh['grp'=8,'lx'=4,'ly'=8] {'lx','ly'}, use_global_device_ids=true, to_apply=%region_9.12 | all-reduce | flops 16 | bytes 128 | tf_op jit(solution)/shard_map/psum | solution.py:53
  549.8 57.8 %all-reduce.12.cloned.1.call-done = f32[4,32768]{1,0:T(4,128)} async-done(((f32[4,32768]{1,0:T(4,128)}), f32[4,32768]{1,0:T(4,128)}) %all-reduce.12.cloned.1.call-update) | async-done | bytes 524304 | tf_op jit(solution)/shard_map/psum | solution.py:22
  607.6 3.5 fusion.103
  611.1 71.6 %psum.162 = f32[4,4]{0,1:T(4,128)S(1)} all-reduce(f32[4,4]{0,1:T(4,128)S(1)} %fusion.103), channel_id=1, replica_groups=mesh['grp'=8,'lx'=4,'ly'=8] {'lx','ly'}, use_global_device_ids=true, to_apply=%region_11.14 | all-reduce | flops 16 | bytes 128 | tf_op jit(solution)/shard_map/psum | solution.py:57
  686.1 73.6 %psum.163 = f32[4,4]{0,1:T(4,128)S(1)} all-reduce(f32[4,4]{0,1:T(4,128)S(1)} %fusion.104), channel_id=1, replica_groups=mesh['grp'=8,'lx'=4,'ly'=8] {'lx','ly'}, use_global_device_ids=true, to_apply=%region_12.15 | all-reduce | flops 16 | bytes 128 | tf_op jit(solution)/shard_map/psum | solution.py:53
  764.0 58.1 %all-reduce.14.cloned.1.call-done = f32[4,32768]{1,0:T(4,128)} async-done(((f32[4,32768]{1,0:T(4,128)}), f32[4,32768]{1,0:T(4,128)}) %all-reduce.14.cloned.1.call-update) | async-done | bytes 524304 | tf_op jit(solution)/shard_map/psum | solution.py:22
  822.1 3.5 fusion.105
  825.6 71.6 %psum.165 = f32[4,4]{0,1:T(4,128)S(1)} all-reduce(f32[4,4]{0,1:T(4,128)S(1)} %fusion.105), channel_id=1, replica_groups=mesh['grp'=8,'lx'=4,'ly'=8] {'lx','ly'}, use_global_device_ids=true, to_apply=%region_14.17 | all-reduce | flops 16 | bytes 128 | tf_op jit(solution)/shard_map/psum | solution.py:57
  900.6 73.6 %psum.166 = f32[4,4]{0,1:T(4,128)S(1)} all-reduce(f32[4,4]{0,1:T(4,128)S(1)} %fusion.106), channel_id=1, replica_groups=mesh['grp'=8,'lx'=4,'ly'=8] {'lx','ly'}, use_global_device_ids=true, to_apply=%region_15.18 | all-reduce | flops 16 | bytes 128 | tf_op jit(solution)/shard_map/psum | solution.py:53
  978.9 57.6 %all-reduce.16.cloned.1.call-done = f32[4,32768]{1,0:T(4,128)} async-done(((f32[4,32768]{1,0:T(4,128)}), f32[4,32768]{1,0:T(4,128)}) %all-reduce.16.cloned.1.call-update) | async-done | bytes 524304 | tf_op jit(solution)/shard_map/psum | solution.py:22
  1036.6 3.5 fusion.107
  1040.0 71.6 %psum.168 = f32[4,4]{0,1:T(4,128)S(1)} all-reduce(f32[4,4]{0,1:T(4,128)S(1)} %fusion.107), channel_id=1, replica_groups=mesh['grp'=8,'lx'=4,'ly'=8] {'lx','ly'}, use_global_device_ids=true, to_apply=%region_17.20 | all-reduce | flops 16 | bytes 128 | tf_op jit(solution)/shard_map/psum | solution.py:57
  1116.0 73.6 %psum.169 = f32[4,4]{0,1:T(4,128)S(1)} all-reduce(f32[4,4]{0,1:T(4,128)S(1)} %fusion.108), channel_id=1, replica_groups=mesh['grp'=8,'lx'=4,'ly'=8] {'lx','ly'}, use_global_device_ids=true, to_apply=%region_18.21 | all-reduce | flops 16 | bytes 128 | tf_op jit(solution)/shard_map/psum | solution.py:53
  1194.2 58.1 %all-reduce.18.cloned.1.call-done = f32[4,32768]{1,0:T(4,128)} async-done(((f32[4,32768]{1,0:T(4,128)}), f32[4,32768]{1,0:T(4,128)}) %all-reduce.18.cloned.1.call-update) | async-done | bytes 524304 | tf_op jit(solution)/shard_map/psum | solution.py:22
  1252.2 3.5 fusion.109
  1255.7 71.6 %psum.171 = f32[4,4]{0,1:T(4,128)S(1)} all-reduce(f32[4,4]{0,1:T(4,128)S(1)} %fusion.109), channel_id=1, replica_groups=mesh['grp'=8,'lx'=4,'ly'=8] {'lx','ly'}, use_global_device_ids=true, to_apply=%region_20.23 | all-reduce | flops 16 | bytes 128 | tf_op jit(solution)/shard_map/psum | solution.py:57
  1331.6 73.8 %psum.172 = f32[4,4]{0,1:T(4,128)S(1)} all-reduce(f32[4,4]{0,1:T(4,128)S(1)} %fusion.110), channel_id=1, replica_groups=mesh['grp'=8,'lx'=4,'ly'=8] {'lx','ly'}, use_global_device_ids=true, to_apply=%region_21.24 | all-reduce | flops 16 | bytes 128 | tf_op jit(solution)/shard_map/psum | solution.py:53
  1409.9 58.1 %all-reduce.20.cloned.1.call-done = f32[4,32768]{1,0:T(4,128)} async-done(((f32[4,32768]{1,0:T(4,128)}), f32[4,32768]{1,0:T(4,128)}) %all-reduce.20.cloned.1.call-update) | async-done | bytes 524304 | tf_op jit(solution)/shard_map/psum | solution.py:22
  1468.0 3.5 fusion.111
  1471.5 71.6 %psum.174 = f32[4,4]{0,1:T(4,128)S(1)} all-reduce(f32[4,4]{0,1:T(4,128)S(1)} %fusion.111), channel_id=1, replica_groups=mesh['grp'=8,'lx'=4,'ly'=8] {'lx','ly'}, use_global_device_ids=true, to_apply=%region_23.26 | all-reduce | flops 16 | bytes 128 | tf_op jit(solution)/shard_map/psum | solution.py:57
  1547.5 73.6 %psum.175 = f32[4,4]{0,1:T(4,128)S(1)} all-reduce(f32[4,4]{0,1:T(4,128)S(1)} %fusion.112), channel_id=1, replica_groups=mesh['grp'=8,'lx'=4,'ly'=8] {'lx','ly'}, use_global_device_ids=true, to_apply=%region_24.27 | all-reduce | flops 16 | bytes 128 | tf_op jit(solution)/shard_map/psum | solution.py:53
  (147 shorter events, 86.7 us)
Async XLA Ops:
  6.5 172.1 %all-reduce.8.cloned.1.call-start = ((), (), s32[]{:S(2)}) async-start(), calls=%async_computation | async-start | bytes 1048576 | tf_op jit(solution)/shard_map/psum | solution.py:22
  7.4 4.5 collective-permute-start
  10.5 8.1 copy-start.6
  10.5 15.1 copy-start
  10.5 4.9 collective-permute-start.1
  16.5 2.1 copy-start.7
  16.5 5.2 collective-permute-start.2
  16.7 9.0 collective-permute-start.3
  26.1 3.7 collective-permute-start.4
  26.2 4.9 collective-permute-start.5
  31.3 6.0 collective-permute-start.6
  34.6 5.1 collective-permute-start.7
  118.0 275.1 %all-reduce.10.cloned.1.call-start = ((), (), s32[]{:S(2)}) async-start(), calls=%async_computation.1 | async-start | bytes 1048576 | tf_op jit(solution)/shard_map/psum | solution.py:22
  178.6 75.1 %copy-start.5 = (f32[4,32768]{1,0:T(4,128)S(1)}, f32[4,32768]{1,0:T(4,128)}, u32[]{:S(2)}) copy-start(f32[4,32768]{1,0:T(4,128)} %all-reduce.8.cloned.1.call-done) | copy-start | bytes 1572868
  335.0 272.6 %all-reduce.12.cloned.1.call-start = ((), (), s32[]{:S(2)}) async-start(), calls=%async_computation.2 | async-start | bytes 1048576 | tf_op jit(solution)/shard_map/psum | solution.py:22
  393.1 75.1 %copy-start.2 = (f32[4,32768]{1,0:T(4,128)S(1)}, f32[4,32768]{1,0:T(4,128)}, u32[]{:S(2)}) copy-start(f32[4,32768]{1,0:T(4,128)} %all-reduce.10.cloned.1.call-done) | copy-start | bytes 1572868
  549.5 272.6 %all-reduce.14.cloned.1.call-start = ((), (), s32[]{:S(2)}) async-start(), calls=%async_computation.3 | async-start | bytes 1048576 | tf_op jit(solution)/shard_map/psum | solution.py:22
  607.6 75.1 %copy-start.3 = (f32[4,32768]{1,0:T(4,128)S(1)}, f32[4,32768]{1,0:T(4,128)}, u32[]{:S(2)}) copy-start(f32[4,32768]{1,0:T(4,128)} %all-reduce.12.cloned.1.call-done) | copy-start | bytes 1572868
  764.0 272.6 %all-reduce.16.cloned.1.call-start = ((), (), s32[]{:S(2)}) async-start(), calls=%async_computation.4 | async-start | bytes 1048576 | tf_op jit(solution)/shard_map/psum | solution.py:22
  822.1 75.1 %copy-start.4 = (f32[4,32768]{1,0:T(4,128)S(1)}, f32[4,32768]{1,0:T(4,128)}, u32[]{:S(2)}) copy-start(f32[4,32768]{1,0:T(4,128)} %all-reduce.14.cloned.1.call-done) | copy-start | bytes 1572868
  978.5 273.7 %all-reduce.18.cloned.1.call-start = ((), (), s32[]{:S(2)}) async-start(), calls=%async_computation.5 | async-start | bytes 1048576 | tf_op jit(solution)/shard_map/psum | solution.py:22
  1194.1 273.9 %all-reduce.20.cloned.1.call-start = ((), (), s32[]{:S(2)}) async-start(), calls=%async_computation.6 | async-start | bytes 1048576 | tf_op jit(solution)/shard_map/psum | solution.py:22
  1545.1 78.4 %copy-start.1 = (f32[4,32768]{1,0:T(4,128)S(1)}, f32[4,32768]{1,0:T(4,128)}, u32[]{:S(2)}) copy-start(f32[4,32768]{1,0:T(4,128)} %convolution_select_fusion.1) | copy-start | bytes 1572868
Sparse Core Ops, SparseCore 0:
  118.2 60.3 all-reduce.7
  335.1 57.9 all-reduce.9
  549.6 57.9 all-reduce.11
  764.1 57.9 all-reduce.13
  978.6 57.9 all-reduce.15
  1194.2 57.9 all-reduce.17
  1410.0 57.9 all-reduce.19
where the time goes:
time: 1640 us; the launch traced here: 1630 us
  blocking collectives  1090 us (66%)
  waiting for transfers between devices  427 us (26%)
  matrix products  69.2 us (4%)
  other arithmetic  19.4 us (1%)
    psum x8, blocking collectives, body(): lax.psum(jnp.dot(flat, flat.T, precision=highest), ('lx', 'ly')) / total  586 us
    psum x7, blocking collectives, body(): lax.psum(jnp.dot(shared, flat.T, precision=highest), ('lx', 'ly')) / total  501 us
    psum x7, waiting for transfers between devices, from_root(): return lax.psum(kept, axis)  408 us
  transfers between devices with their start and end apart: 15, of which 15 were waited for; matrix products, arithmetic and copies ran while one was open for 0% of the time, Pallas kernels for 0%

commit v1 on v0

--- a/solution.py
+++ b/solution.py
@@ -54,7 +54,10 @@
         done = jnp.dot(lower_inverse(gram), flat, precision=highest)
         result = jnp.where(mine == h, done, result)
         shared = from_root(done, "grp", h)
-        coeff = lax.psum(jnp.dot(shared, flat.T, precision=highest), ("lx", "ly")) / total
+        coeff = (
+            jnp.sum(lax.all_gather(jnp.dot(shared, flat.T, precision=highest), ("lx", "ly")), 0)
+            / total
+        )
         later = mine > h
         flat = jnp.where(later, flat - jnp.dot(coeff.T, shared, precision=highest), flat)
     return result.reshape(count_vec, rows_local, cols_local)

time: 1640 us -> 1470 us (0.90)
  blocking collectives: 1090 us -> 910 us
    psum x7 -> x0, blocking collectives: 501 us -> none  [body(): lax.psum(jnp.dot(shared, flat.T, precision=highest), ('lx', 'ly')) / total]
    all_gather x0 -> x7, blocking collectives: none -> 342 us  [body(): lax.all_gather(jnp.dot(shared, flat.T, precision=highest), ('lx', 'ly'))]
    psum x8, blocking collectives: 586 us -> 568 us  [body(): lax.psum(jnp.dot(flat, flat.T, precision=highest), ('lx', 'ly')) / total]
where the time goes in v1:
time: 1470 us; the launch traced here: 1460 us
  blocking collectives  910 us (62%)
  waiting for transfers between devices  433 us (29%)
  matrix products  69.8 us (5%)
  other arithmetic  19.7 us (1%)
  between operations  15.3 us (1%)
    psum x8, blocking collectives, body(): lax.psum(jnp.dot(flat, flat.T, precision=highest), ('lx', 'ly')) / total  568 us
    psum x7, waiting for transfers between devices, from_root(): return lax.psum(kept, axis)  415 us
    all_gather x7, blocking collectives, body(): lax.all_gather(jnp.dot(shared, flat.T, precision=highest), ('lx', 'ly'))  342 us
  transfers between devices with their start and end apart: 15, of which 15 were waited for; matrix products, arithmetic and copies ran while one was open for 0% of the time, Pallas kernels for 0%

profile of v1, /device:TPU:32, one launch (start us, length us, event | category | flops | bytes accessed | tf_op | source)
XLA Modules:
  0.0 1463.1 jit_solution(9946818929637149135)
XLA Ops:
  11.9 3.5 collective-permute-done.1
  21.7 3.9 collective-permute-done.3
  31.3 3.3 collective-permute-start.6
  42.6 71.0 %psum.105 = f32[4,4]{0,1:T(4,128)S(1)} all-reduce(f32[4,4]{0,1:T(4,128)S(1)} %convolution_bitcast_fusion.7), channel_id=1, replica_groups=mesh['grp'=8,'lx'=4,'ly'=8] {'lx','ly'}, use_global_device_ids=true, to_apply=%region_1.2 | all-reduce | flops 16 | bytes 128 | tf_op jit(solution)/shard_map/psum | solution.py:53
  118.3 60.3 %all-reduce.8.cloned.1.call-done = f32[4,32768]{1,0:T(4,128)} async-done(((f32[4,32768]{1,0:T(4,128)}), f32[4,32768]{1,0:T(4,128)}) %all-reduce.8.cloned.1.call-update) | async-done | bytes 524304 | tf_op jit(solution)/shard_map/psum | solution.py:22
  178.6 3.6 convolution_bitcast_fusion.6
  182.2 48.8 %all-gather.7 = f32[32,4,4]{2,1,0:T(4,128)S(1)} all-gather(f32[1,4,4]{2,1,0:T(4,128)S(1)} %convolution_bitcast_fusion.6), channel_id=2, replica_groups=mesh['grp'=8,'lx'=4,'ly'=8] {'lx','ly'}, dimensions={0}, use_global_device_ids=true | all-gather | bytes 2112 | tf_op jit(solution)/shard_map/all_gather | solution.py:58
  234.5 71.0 %psum.107 = f32[4,4]{0,1:T(4,128)S(1)} all-reduce(f32[4,4]{0,1:T(4,128)S(1)} %fusion.99), channel_id=1, replica_groups=mesh['grp'=8,'lx'=4,'ly'=8] {'lx','ly'}, use_global_device_ids=true, to_apply=%region_6.9 | all-reduce | flops 16 | bytes 128 | tf_op jit(solution)/shard_map/psum | solution.py:53
  309.9 59.2 %all-reduce.10.cloned.1.call-done = f32[4,32768]{1,0:T(4,128)} async-done(((f32[4,32768]{1,0:T(4,128)}), f32[4,32768]{1,0:T(4,128)}) %all-reduce.10.cloned.1.call-update) | async-done | bytes 524304 | tf_op jit(solution)/shard_map/psum | solution.py:22
  369.0 3.6 convolution_bitcast_fusion.5
  372.6 48.8 %all-gather.8 = f32[32,4,4]{2,1,0:T(4,128)S(1)} all-gather(f32[1,4,4]{2,1,0:T(4,128)S(1)} %convolution_bitcast_fusion.5), channel_id=3, replica_groups=mesh['grp'=8,'lx'=4,'ly'=8] {'lx','ly'}, dimensions={0}, use_global_device_ids=true | all-gather | bytes 2112 | tf_op jit(solution)/shard_map/all_gather | solution.py:58
  424.9 71.0 %psum.109 = f32[4,4]{0,1:T(4,128)S(1)} all-reduce(f32[4,4]{0,1:T(4,128)S(1)} %fusion.100), channel_id=1, replica_groups=mesh['grp'=8,'lx'=4,'ly'=8] {'lx','ly'}, use_global_device_ids=true, to_apply=%region_9.12 | all-reduce | flops 16 | bytes 128 | tf_op jit(solution)/shard_map/psum | solution.py:53
  500.5 59.0 %all-reduce.12.cloned.1.call-done = f32[4,32768]{1,0:T(4,128)} async-done(((f32[4,32768]{1,0:T(4,128)}), f32[4,32768]{1,0:T(4,128)}) %all-reduce.12.cloned.1.call-update) | async-done | bytes 524304 | tf_op jit(solution)/shard_map/psum | solution.py:22
  559.4 3.6 convolution_bitcast_fusion.4
  563.0 48.8 %all-gather.9 = f32[32,4,4]{2,1,0:T(4,128)S(1)} all-gather(f32[1,4,4]{2,1,0:T(4,128)S(1)} %convolution_bitcast_fusion.4), channel_id=4, replica_groups=mesh['grp'=8,'lx'=4,'ly'=8] {'lx','ly'}, dimensions={0}, use_global_device_ids=true | all-gather | bytes 2112 | tf_op jit(solution)/shard_map/all_gather | solution.py:58
  615.3 71.0 %psum.111 = f32[4,4]{0,1:T(4,128)S(1)} all-reduce(f32[4,4]{0,1:T(4,128)S(1)} %fusion.101), channel_id=1, replica_groups=mesh['grp'=8,'lx'=4,'ly'=8] {'lx','ly'}, use_global_device_ids=true, to_apply=%region_12.15 | all-reduce | flops 16 | bytes 128 | tf_op jit(solution)/shard_map/psum | solution.py:53
  690.7 59.2 %all-reduce.14.cloned.1.call-done = f32[4,32768]{1,0:T(4,128)} async-done(((f32[4,32768]{1,0:T(4,128)}), f32[4,32768]{1,0:T(4,128)}) %all-reduce.14.cloned.1.call-update) | async-done | bytes 524304 | tf_op jit(solution)/shard_map/psum | solution.py:22
  749.8 3.6 convolution_bitcast_fusion.3
  753.4 48.8 %all-gather.10 = f32[32,4,4]{2,1,0:T(4,128)S(1)} all-gather(f32[1,4,4]{2,1,0:T(4,128)S(1)} %convolution_bitcast_fusion.3), channel_id=5, replica_groups=mesh['grp'=8,'lx'=4,'ly'=8] {'lx','ly'}, dimensions={0}, use_global_device_ids=true | all-gather | bytes 2112 | tf_op jit(solution)/shard_map/all_gather | solution.py:58
  805.7 71.0 %psum.113 = f32[4,4]{0,1:T(4,128)S(1)} all-reduce(f32[4,4]{0,1:T(4,128)S(1)} %fusion.102), channel_id=1, replica_groups=mesh['grp'=8,'lx'=4,'ly'=8] {'lx','ly'}, use_global_device_ids=true, to_apply=%region_15.18 | all-reduce | flops 16 | bytes 128 | tf_op jit(solution)/shard_map/psum | solution.py:53
  881.5 58.8 %all-reduce.16.cloned.1.call-done = f32[4,32768]{1,0:T(4,128)} async-done(((f32[4,32768]{1,0:T(4,128)}), f32[4,32768]{1,0:T(4,128)}) %all-reduce.16.cloned.1.call-update) | async-done | bytes 524304 | tf_op jit(solution)/shard_map/psum | solution.py:22
  940.2 3.5 convolution_bitcast_fusion.2
  943.7 48.8 %all-gather.11 = f32[32,4,4]{2,1,0:T(4,128)S(1)} all-gather(f32[1,4,4]{2,1,0:T(4,128)S(1)} %convolution_bitcast_fusion.2), channel_id=6, replica_groups=mesh['grp'=8,'lx'=4,'ly'=8] {'lx','ly'}, dimensions={0}, use_global_device_ids=true | all-gather | bytes 2112 | tf_op jit(solution)/shard_map/all_gather | solution.py:58
  997.1 71.0 %psum.115 = f32[4,4]{0,1:T(4,128)S(1)} all-reduce(f32[4,4]{0,1:T(4,128)S(1)} %fusion.103), channel_id=1, replica_groups=mesh['grp'=8,'lx'=4,'ly'=8] {'lx','ly'}, use_global_device_ids=true, to_apply=%region_18.21 | all-reduce | flops 16 | bytes 128 | tf_op jit(solution)/shard_map/psum | solution.py:53
  1072.6 59.2 %all-reduce.18.cloned.1.call-done = f32[4,32768]{1,0:T(4,128)} async-done(((f32[4,32768]{1,0:T(4,128)}), f32[4,32768]{1,0:T(4,128)}) %all-reduce.18.cloned.1.call-update) | async-done | bytes 524304 | tf_op jit(solution)/shard_map/psum | solution.py:22
  1131.8 3.5 convolution_bitcast_fusion.1
  1135.3 48.8 %all-gather.12 = f32[32,4,4]{2,1,0:T(4,128)S(1)} all-gather(f32[1,4,4]{2,1,0:T(4,128)S(1)} %convolution_bitcast_fusion.1), channel_id=7, replica_groups=mesh['grp'=8,'lx'=4,'ly'=8] {'lx','ly'}, dimensions={0}, use_global_device_ids=true | all-gather | bytes 2112 | tf_op jit(solution)/shard_map/all_gather | solution.py:58
  1188.6 71.2 %psum.117 = f32[4,4]{0,1:T(4,128)S(1)} all-reduce(f32[4,4]{0,1:T(4,128)S(1)} %fusion.104), channel_id=1, replica_groups=mesh['grp'=8,'lx'=4,'ly'=8] {'lx','ly'}, use_global_device_ids=true, to_apply=%region_21.24 | all-reduce | flops 16 | bytes 128 | tf_op jit(solution)/shard_map/psum | solution.py:53
  1264.3 59.3 %all-reduce.20.cloned.1.call-done = f32[4,32768]{1,0:T(4,128)} async-done(((f32[4,32768]{1,0:T(4,128)}), f32[4,32768]{1,0:T(4,128)}) %all-reduce.20.cloned.1.call-update) | async-done | bytes 524304 | tf_op jit(solution)/shard_map/psum | solution.py:22
  1323.5 3.5 convolution_bitcast_fusion
  1327.1 48.8 %all-gather.13 = f32[32,4,4]{2,1,0:T(4,128)S(1)} all-gather(f32[1,4,4]{2,1,0:T(4,128)S(1)} %convolution_bitcast_fusion), channel_id=8, replica_groups=mesh['grp'=8,'lx'=4,'ly'=8] {'lx','ly'}, dimensions={0}, use_global_device_ids=true | all-gather | bytes 2112 | tf_op jit(solution)/shard_map/all_gather | solution.py:58
  1380.4 71.0 %psum.119 = f32[4,4]{0,1:T(4,128)S(1)} all-reduce(f32[4,4]{0,1:T(4,128)S(1)} %fusion.105), channel_id=1, replica_groups=mesh['grp'=8,'lx'=4,'ly'=8] {'lx','ly'}, use_global_device_ids=true, to_apply=%region_24.27 | all-reduce | flops 16 | bytes 128 | tf_op jit(solution)/shard_map/psum | solution.py:53
  (161 shorter events, 87.7 us)
Async XLA Ops:
  6.5 172.1 %all-reduce.8.cloned.1.call-start = ((), (), s32[]{:S(2)}) async-start(), calls=%async_computation | async-start | bytes 1048576 | tf_op jit(solution)/shard_map/psum | solution.py:22
  7.4 4.5 collective-permute-start
  10.5 8.1 copy-start.6
  10.5 15.1 %copy-start = (f32[4,64,512]{2,1,0:T(8,128)S(1)}, f32[4,64,512]{2,1,0:T(8,128)}, u32[]{:S(2)}) copy-start(f32[4,64,512]{2,1,0:T(8,128)} %param.8) | copy-start | bytes 1572868
  10.5 4.9 collective-permute-start.1
  16.5 2.1 copy-start.7
  16.5 5.2 collective-permute-start.2
  16.7 9.0 collective-permute-start.3
  26.1 3.7 collective-permute-start.4
  26.2 4.9 collective-permute-start.5
  31.3 6.0 collective-permute-start.6
  34.6 5.1 collective-permute-start.7
  118.0 251.0 %all-reduce.10.cloned.1.call-start = ((), (), s32[]{:S(2)}) async-start(), calls=%async_computation.1 | async-start | bytes 1048576 | tf_op jit(solution)/shard_map/psum | solution.py:22
  178.6 52.5 %copy-start.5 = (f32[4,32768]{1,0:T(4,128)S(1)}, f32[4,32768]{1,0:T(4,128)}, u32[]{:S(2)}) copy-start(f32[4,32768]{1,0:T(4,128)} %all-reduce.8.cloned.1.call-done) | copy-start | bytes 1572868
  309.8 249.6 %all-reduce.12.cloned.1.call-start = ((), (), s32[]{:S(2)}) async-start(), calls=%async_computation.2 | async-start | bytes 1048576 | tf_op jit(solution)/shard_map/psum | solution.py:22
  369.0 52.5 %copy-start.2 = (f32[4,32768]{1,0:T(4,128)S(1)}, f32[4,32768]{1,0:T(4,128)}, u32[]{:S(2)}) copy-start(f32[4,32768]{1,0:T(4,128)} %all-reduce.10.cloned.1.call-done) | copy-start | bytes 1572868
  500.2 249.6 %all-reduce.14.cloned.1.call-start = ((), (), s32[]{:S(2)}) async-start(), calls=%async_computation.3 | async-start | bytes 1048576 | tf_op jit(solution)/shard_map/psum | solution.py:22
  559.4 52.5 %copy-start.3 = (f32[4,32768]{1,0:T(4,128)S(1)}, f32[4,32768]{1,0:T(4,128)}, u32[]{:S(2)}) copy-start(f32[4,32768]{1,0:T(4,128)} %all-reduce.12.cloned.1.call-done) | copy-start | bytes 1572868
  690.6 249.6 %all-reduce.16.cloned.1.call-start = ((), (), s32[]{:S(2)}) async-start(), calls=%async_computation.4 | async-start | bytes 1048576 | tf_op jit(solution)/shard_map/psum | solution.py:22
  749.8 52.5 %copy-start.4 = (f32[4,32768]{1,0:T(4,128)S(1)}, f32[4,32768]{1,0:T(4,128)}, u32[]{:S(2)}) copy-start(f32[4,32768]{1,0:T(4,128)} %all-reduce.14.cloned.1.call-done) | copy-start | bytes 1572868
  881.0 250.8 %all-reduce.18.cloned.1.call-start = ((), (), s32[]{:S(2)}) async-start(), calls=%async_computation.5 | async-start | bytes 1048576 | tf_op jit(solution)/shard_map/psum | solution.py:22
  1072.5 251.0 %all-reduce.20.cloned.1.call-start = ((), (), s32[]{:S(2)}) async-start(), calls=%async_computation.6 | async-start | bytes 1048576 | tf_op jit(solution)/shard_map/psum | solution.py:22
  1378.0 75.8 %copy-start.1 = (f32[4,32768]{1,0:T(4,128)S(1)}, f32[4,32768]{1,0:T(4,128)}, u32[]{:S(2)}) copy-start(f32[4,32768]{1,0:T(4,128)} %convolution_select_fusion.1) | copy-start | bytes 1572868
Sparse Core Ops, SparseCore 0:
  118.2 60.3 all-reduce.7
  309.9 59.0 all-reduce.9
  500.3 59.0 all-reduce.11
  690.7 59.0 all-reduce.13
  881.1 59.0 all-reduce.15
  1072.7 59.0 all-reduce.17
  1264.4 59.1 all-reduce.19
